TPU v7x, 32 devices: a whole 2x2x4 slice. The times are simulated.
32 devices in a mesh: wide: 16 (over z, x, core), narrow: 2 (over y).
Axes of the slice: x: 2, y: 2, z: 4, core: 2. Of those that a mesh axis runs over, the one named last changes fastest.
Arguments:
- tokens: bfloat16 [16384, 768], P(('wide', 'narrow')), may hold values from -6 to 6
- token_marks: int32 [16384], P(('wide', 'narrow')), may hold values 0 or 1
- crop_lengths: int32 [256], P('wide'), may hold values from 0 to 576, as said below
- bucket_ids: int32 [256], P('wide'), may hold values from 0 to 3
- mask_token: bfloat16 [768], replicated, may hold values from -5 to 5
- norm1_gain: bfloat16 [768], replicated, may hold values from 0.099609375 to 1.8984375
- norm1_bias: bfloat16 [768], replicated, may hold values from -3 to 3
- w_qkv: bfloat16 [3, 768, 768], P(None, None, 'narrow'), may hold values from -0.21875 to 0.21875
- qv_bias: bfloat16 [2, 768], P(None, 'narrow'), may hold values from -3 to 3
- w_proj: bfloat16 [768, 768], P('narrow'), may hold values from -1.75 to 1.75
- proj_bias: bfloat16 [768], replicated, may hold values from -3 to 3
- scale_attn: bfloat16 [768], replicated, may hold values from 0.5 to 1.5
- norm2_gain: bfloat16 [768], replicated, may hold values from 0.099609375 to 1.8984375
- norm2_bias: bfloat16 [768], replicated, may hold values from -3 to 3
- w_fc1: bfloat16 [768, 3072], P(None, 'narrow'), may hold values from -0.21875 to 0.21875
- fc1_bias: bfloat16 [3072], P('narrow'), may hold values from -3 to 3
- w_fc2: bfloat16 [3072, 768], P('narrow'), may hold values from -0.109375 to 0.109375
- fc2_bias: bfloat16 [768], replicated, may hold values from -3 to 3
- scale_mlp: bfloat16 [768], replicated, may hold values from 0.5 to 1.5
- cotangent: bfloat16 [16384, 768], P(('wide', 'narrow')), may hold values from -6 to 6
Outputs:
- output: bfloat16 [16384, 768], P(('wide', 'narrow'))
- grad_tokens: float32 [16384, 768], P(('wide', 'narrow'))
- grad_mask_token: float32 [768], replicated
- grad_norm1_gain: float32 [768], replicated
- grad_norm1_bias: float32 [768], replicated
- grad_qkv: float32 [3, 768, 768], P(None, None, 'narrow')
- grad_qv_bias: float32 [2, 768], P(None, 'narrow')
- grad_proj: float32 [768, 768], P('narrow')
- grad_proj_bias: float32 [768], replicated
- grad_scale_attn: float32 [768], replicated
- grad_norm2_gain: float32 [768], replicated
- grad_norm2_bias: float32 [768], replicated
- grad_fc1: float32 [768, 3072], P(None, 'narrow')
- grad_fc1_bias: float32 [3072], P('narrow')
- grad_fc2: float32 [3072, 768], P('narrow')
- grad_fc2_bias: float32 [768], replicated
- grad_scale_mlp: float32 [768], replicated
Inputs may be any that keep to these rules, and one draw needn't show every extreme that they name: `crop_lengths`: length 0 marks an empty slot. The nonempty slots of a buffer come first, and their padded rows together fill at most 1024; some buffer is filled to exactly 1024 rows. A nonempty crop has more than 48 rows, and its bucket is the smallest of 64, 144, 256, 576 that holds it.
All inputs are finite; a program needn't handle non-finite values. No bound on the sum of `token_marks` on one device may be relied on, other than what follows from the above.
Results may differ from a plain program's by a relative error of at most 0.017.
Values may be sent and summed in bfloat16 or wider, within the bound.
No kernel may reach another device: no remote copies, remote signals or barrier semaphores. Data moves between devices by JAX's collectives and lax.ppermute only.
A program may use at most 128 MiB of HBM per device.

v0:
```python
from functools import partial
import jax
import jax.numpy as jnp
from jax import lax
from jax.sharding import PartitionSpec as P

HEAD_DIM = 64
B0 = 64
B1 = 144
B2 = 256
B3 = 576
epsilon = 1e-06
score_scale = 0.125
masked_score = -1e30


def layer_norm(values_in, norm_gain, norm_shift):
    row_mean = jnp.mean(values_in, axis=-1, keepdims=True)
    centered = values_in - row_mean
    variance = jnp.mean(centered * centered, axis=-1, keepdims=True)
    return centered * lax.rsqrt(variance + epsilon) * norm_gain + norm_shift


def row_layout(lengths, buckets, row_total):
    slot_count = lengths.shape[0]
    bucket_rows = jnp.where(
        buckets == 0, B0, jnp.where(buckets == 1, B1, jnp.where(buckets == 2, B2, B3))
    )
    padded_sizes = jnp.where(lengths > 0, bucket_rows, 0).astype(jnp.int32)
    slot_ends = jnp.cumsum(padded_sizes)
    starts = slot_ends - padded_sizes
    row_ids = jnp.arange(row_total, dtype=jnp.int32)
    crop_of_row = jnp.sum((row_ids[:, None] >= slot_ends[None, :]).astype(jnp.int32), axis=1)
    slot_match = crop_of_row[:, None] == jnp.arange(slot_count, dtype=jnp.int32)[None, :]
    row_start = jnp.sum(jnp.where(slot_match, starts[None, :], 0), axis=1)
    row_length = jnp.sum(jnp.where(slot_match, lengths[None, :], 0), axis=1)
    is_valid = (crop_of_row < slot_count) & (row_ids - row_start < row_length)
    return (crop_of_row, is_valid)


def allowed_block(crop_of_row, is_valid, first_row, block_rows):
    row_total = crop_of_row.shape[0]
    query_crop = lax.dynamic_slice_in_dim(crop_of_row, first_row, block_rows)
    query_valid = lax.dynamic_slice_in_dim(is_valid, first_row, block_rows)
    query_ids = first_row + jnp.arange(block_rows, dtype=jnp.int32)
    key_ids = jnp.arange(row_total, dtype=jnp.int32)
    same_crop = (
        (query_crop[:, None] == crop_of_row[None, :]) & query_valid[:, None] & is_valid[None, :]
    )
    itself = (query_ids[:, None] == key_ids[None, :]) & jnp.logical_not(query_valid)[:, None]
    return same_crop | itself


def block_rows_for():
    return 512


def slab(matrix, first_row, row_count):
    return lax.dynamic_slice_in_dim(matrix, first_row, row_count, 0)


def shards(
    tokens,
    token_marks,
    crop_lengths,
    bucket_ids,
    mask_token,
    norm1_gain,
    norm1_bias,
    w_qkv,
    qv_bias,
    w_proj,
    proj_bias,
    scale_attn,
    norm2_gain,
    norm2_bias,
    w_fc1,
    fc1_bias,
    w_fc2,
    fc2_bias,
    scale_mlp,
    cotangent,
):
    own_rows = tokens.shape[0]
    row_total = own_rows * lax.axis_size("narrow")
    first_own = lax.axis_index("narrow") * own_rows
    crop_of_row, is_valid = row_layout(crop_lengths, bucket_ids, row_total)
    own_valid = lax.dynamic_slice_in_dim(is_valid, first_own, own_rows)[:, None]
    marked = (token_marks == 1)[:, None]
    gain1 = norm1_gain.astype(jnp.float32)
    shift1 = norm1_bias.astype(jnp.float32)
    gain2 = norm2_gain.astype(jnp.float32)
    shift2 = norm2_bias.astype(jnp.float32)
    scale1 = scale_attn.astype(jnp.float32)
    scale2 = scale_mlp.astype(jnp.float32)
    x_in = jnp.where(marked, mask_token.astype(jnp.float32)[None, :], tokens.astype(jnp.float32))
    normed1 = layer_norm(x_in, gain1, shift1).astype(jnp.bfloat16)
    normed1_all = lax.all_gather(normed1, "narrow", axis=0, tiled=True)
    projected = jnp.einsum("rd,cde->cre", normed1_all, w_qkv, preferred_element_type=jnp.float32)
    bias_pair = qv_bias.astype(jnp.float32)
    queries = (projected[0] + bias_pair[0]).astype(jnp.bfloat16)
    keys_all = projected[1].astype(jnp.bfloat16)
    values_all = (projected[2] + bias_pair[1]).astype(jnp.bfloat16)
    heads_local = queries.shape[1] // HEAD_DIM
    query_heads = queries.reshape(row_total, heads_local, HEAD_DIM)
    key_heads = keys_all.reshape(row_total, heads_local, HEAD_DIM)
    value_heads = values_all.reshape(row_total, heads_local, HEAD_DIM)
    block_rows = block_rows_for()
    block_count = row_total // block_rows
    block_ids = jnp.arange(block_count, dtype=jnp.int32)

    def attend(block_index):
        first_row = block_index * block_rows
        query_block = slab(query_heads, first_row, block_rows)
        scores = (
            jnp.einsum("qhd,khd->hqk", query_block, key_heads, preferred_element_type=jnp.float32)
            * score_scale
        )
        allowed = allowed_block(crop_of_row, is_valid, first_row, block_rows)
        scores = jnp.where(allowed[None], scores, masked_score)
        row_peak = jnp.max(scores, axis=-1, keepdims=True)
        exponent = jnp.exp(scores - row_peak)
        denominator = jnp.sum(exponent, axis=-1, keepdims=True)
        probability = (exponent / denominator).astype(jnp.bfloat16)
        mixed = jnp.einsum(
            "hqk,khd->qhd", probability, value_heads, preferred_element_type=jnp.float32
        ).astype(jnp.bfloat16)
        return (mixed, (row_peak + jnp.log(denominator))[..., 0])

    mixed_blocks, log_totals = lax.map(attend, block_ids)
    heads_out = mixed_blocks.reshape(row_total, heads_local * HEAD_DIM)
    attn_out = lax.psum_scatter(
        jnp.dot(
            slab(heads_out, jnp.int32(0), own_rows * lax.axis_size("narrow")),
            w_proj,
            preferred_element_type=jnp.float32,
        ).astype(jnp.bfloat16),
        "narrow",
        scatter_dimension=0,
        tiled=True,
    ).astype(jnp.float32) + proj_bias.astype(jnp.float32)
    hidden = x_in + scale1 * attn_out
    normed2 = layer_norm(hidden, gain2, shift2).astype(jnp.bfloat16)
    normed2_all = lax.all_gather(normed2, "narrow", axis=0, tiled=True)
    pre_act = jnp.dot(normed2_all, w_fc1, preferred_element_type=jnp.float32) + fc1_bias.astype(
        jnp.float32
    )
    gelu_exact = partial(jax.nn.gelu, approximate=False)
    activated = gelu_exact(pre_act).astype(jnp.bfloat16)
    branch = lax.psum_scatter(
        jnp.dot(
            slab(activated, jnp.int32(0), own_rows * lax.axis_size("narrow")),
            w_fc2,
            preferred_element_type=jnp.float32,
        ).astype(jnp.bfloat16),
        "narrow",
        scatter_dimension=0,
        tiled=True,
    ).astype(jnp.float32) + fc2_bias.astype(jnp.float32)
    output = jnp.where(own_valid, hidden + scale2 * branch, 0.0).astype(jnp.bfloat16)
    grad_out = jnp.where(own_valid, cotangent.astype(jnp.float32), 0.0)
    grad_branch = (scale2 * grad_out).astype(jnp.bfloat16)
    grad_scale_mlp = jnp.sum(grad_out * branch, axis=0)
    grad_fc2_bias = jnp.sum(grad_branch.astype(jnp.float32), axis=0)
    grad_branch_all = lax.all_gather(grad_branch, "narrow", axis=0, tiled=True)
    grad_fc2 = jnp.einsum(
        "rf,rd->fd", activated, grad_branch_all, preferred_element_type=jnp.float32
    )
    grad_act = jnp.einsum("rd,fd->rf", grad_branch_all, w_fc2, preferred_element_type=jnp.float32)
    gelu_unused, gelu_back = jax.vjp(gelu_exact, pre_act)
    grad_pre = gelu_back(grad_act)[0].astype(jnp.bfloat16)
    grad_fc1_bias = jnp.sum(grad_pre.astype(jnp.float32), axis=0)
    grad_fc1 = jnp.einsum("rd,rf->df", normed2_all, grad_pre, preferred_element_type=jnp.float32)
    grad_normed2 = lax.psum_scatter(
        jnp.einsum(
            "rf,df->rd",
            slab(grad_pre, jnp.int32(0), own_rows * lax.axis_size("narrow")),
            w_fc1,
            preferred_element_type=jnp.float32,
        ).astype(jnp.bfloat16),
        "narrow",
        scatter_dimension=0,
        tiled=True,
    ).astype(jnp.float32)
    norm2_unused, norm2_back = jax.vjp(layer_norm, hidden, gain2, shift2)
    grad_hidden_part, grad_norm2_gain, grad_norm2_bias = norm2_back(grad_normed2)
    grad_hidden = grad_out + grad_hidden_part
    grad_attn = (scale1 * grad_hidden).astype(jnp.bfloat16)
    grad_scale_attn = jnp.sum(grad_hidden * attn_out, axis=0)
    grad_proj_bias = jnp.sum(grad_attn.astype(jnp.float32), axis=0)
    grad_attn_all = lax.all_gather(grad_attn, "narrow", axis=0, tiled=True)
    grad_proj = jnp.einsum(
        "re,rd->ed", heads_out, grad_attn_all, preferred_element_type=jnp.float32
    )
    grad_heads = jnp.einsum(
        "rd,ed->re", grad_attn_all, w_proj, preferred_element_type=jnp.float32
    ).astype(jnp.bfloat16)
    grad_heads = grad_heads.reshape(row_total, heads_local, HEAD_DIM)

    def attend_back(carried, block_index):
        key_sum, value_sum = carried
        first_row = block_index * block_rows
        query_block = slab(query_heads, first_row, block_rows)
        grad_block = slab(grad_heads, first_row, block_rows)
        log_block = log_totals[block_index]
        scores = (
            jnp.einsum("qhd,khd->hqk", query_block, key_heads, preferred_element_type=jnp.float32)
            * score_scale
        )
        allowed = allowed_block(crop_of_row, is_valid, first_row, block_rows)
        exact_probs = jnp.where(
            allowed[None],
            jnp.exp(jnp.where(allowed[None], scores, masked_score) - log_block[..., None]),
            0.0,
        )
        rounded = exact_probs.astype(jnp.bfloat16)
        value_sum = value_sum + jnp.einsum(
            "hqk,qhd->khd", rounded, grad_block, preferred_element_type=jnp.float32
        )
        grad_probs = jnp.einsum(
            "qhd,khd->hqk", grad_block, value_heads, preferred_element_type=jnp.float32
        )
        row_inner = jnp.sum(exact_probs * grad_probs, axis=-1, keepdims=True)
        grad_scores = (exact_probs * (grad_probs - row_inner)).astype(jnp.bfloat16)
        grad_query = (
            jnp.einsum("hqk,khd->qhd", grad_scores, key_heads, preferred_element_type=jnp.float32)
            * score_scale
        )
        key_sum = (
            key_sum
            + jnp.einsum(
                "hqk,qhd->khd", grad_scores, query_block, preferred_element_type=jnp.float32
            )
            * score_scale
        )
        return ((key_sum, value_sum), grad_query)

    zero_heads = jnp.zeros((row_total, heads_local, HEAD_DIM), jnp.float32)
    (key_sum, value_sum), query_blocks = lax.scan(attend_back, (zero_heads, zero_heads), block_ids)
    width_local = heads_local * HEAD_DIM
    grad_queries = query_blocks.reshape(row_total, width_local).astype(jnp.bfloat16)
    grad_keys = key_sum.reshape(row_total, width_local).astype(jnp.bfloat16)
    grad_values = value_sum.reshape(row_total, width_local).astype(jnp.bfloat16)
    grad_stack = jnp.stack([grad_queries, grad_keys, grad_values])
    grad_qkv = jnp.einsum(
        "rd,cre->cde", normed1_all, grad_stack, preferred_element_type=jnp.float32
    )
    grad_qv_bias = jnp.stack(
        [
            jnp.sum(grad_queries.astype(jnp.float32), axis=0),
            jnp.sum(grad_values.astype(jnp.float32), axis=0),
        ]
    )
    grad_qkv, grad_qv_bias, grad_proj, grad_fc1, grad_fc1_bias, grad_fc2 = lax.psum(
        (grad_qkv, grad_qv_bias, grad_proj, grad_fc1, grad_fc1_bias, grad_fc2), "wide"
    )
    grad_normed1 = lax.psum_scatter(
        jnp.einsum("cre,cde->rd", grad_stack, w_qkv, preferred_element_type=jnp.float32).astype(
            jnp.bfloat16
        ),
        "narrow",
        scatter_dimension=0,
        tiled=True,
    ).astype(jnp.float32)
    norm1_unused, norm1_back = jax.vjp(layer_norm, x_in, gain1, shift1)
    grad_x_part, grad_norm1_gain, grad_norm1_bias = norm1_back(grad_normed1)
    grad_x_in = grad_hidden + grad_x_part
    grad_tokens = jnp.where(marked, 0.0, grad_x_in)
    grad_mask_token = jnp.sum(jnp.where(marked, grad_x_in, 0.0), axis=0)
    (
        grad_mask_token,
        grad_norm1_gain,
        grad_norm1_bias,
        grad_proj_bias,
        grad_scale_attn,
        grad_norm2_gain,
        grad_norm2_bias,
        grad_fc2_bias,
        grad_scale_mlp,
    ) = lax.psum(
        (
            grad_mask_token,
            grad_norm1_gain,
            grad_norm1_bias,
            grad_proj_bias,
            grad_scale_attn,
            grad_norm2_gain,
            grad_norm2_bias,
            grad_fc2_bias,
            grad_scale_mlp,
        ),
        ("wide", "narrow"),
    )
    return (
        output,
        grad_tokens,
        grad_mask_token,
        grad_norm1_gain,
        grad_norm1_bias,
        grad_qkv,
        grad_qv_bias,
        grad_proj,
        grad_proj_bias,
        grad_scale_attn,
        grad_norm2_gain,
        grad_norm2_bias,
        grad_fc1,
        grad_fc1_bias,
        grad_fc2,
        grad_fc2_bias,
        grad_scale_mlp,
    )


def solution(mesh):
    return jax.shard_map(
        shards,
        mesh=mesh,
        in_specs=(
            P(("wide", "narrow"), None),
            P(("wide", "narrow")),
            P("wide"),
            P("wide"),
            P(),
            P(),
            P(),
            P(None, None, "narrow"),
            P(None, "narrow"),
            P("narrow", None),
            P(),
            P(),
            P(),
            P(),
            P(None, "narrow"),
            P("narrow"),
            P("narrow", None),
            P(),
            P(),
            P(("wide", "narrow"), None),
        ),
        out_specs=(
            P(("wide", "narrow"), None),
            P(("wide", "narrow"), None),
            P(),
            P(),
            P(),
            P(None, None, "narrow"),
            P(None, "narrow"),
            P("narrow", None),
            P(),
            P(),
            P(),
            P(),
            P(None, "narrow"),
            P("narrow"),
            P("narrow", None),
            P(),
            P(),
        ),
        check_vma=False,
    )
```

profile of v0, /device:TPU:0, one launch (start us, length us, event | category | flops | bytes accessed | tf_op | source)
XLA Modules:
  0.0 672.5 jit_solution(14743792329770781047)
XLA Ops:
  15.7 29.3 %all-gather.5.cloned.1.call-done = bf16[1024,768]{1,0:T(8,128)(2,1)} async-done(((bf16[512,768]{1,0:T(8,128)(2,1)}), bf16[1024,768]{1,0:T(8,128)(2,1)}) %all-gather.5.cloned.1.call-update) | async-done | bytes 1572880 | tf_op jit(solution)/shard_map/all_gather | solution.py:98
  45.0 4.0 convolution_bitcast_fusion
  50.9 29.5 %while.27 = (s32[]{:T(128)}, bf16[2,512,6,64]{1,3,2,0:T(8,128)(2,1)}, f32[2,6,512]{2,1,0:T(8,128)S(1)}, s32[2]{0:T(128)S(1)}, s32[1024]{0:T(1024)S(1)}, /*index=...) while((s32[]{:T(128)}, ...), condition=%wide.region_9.10_spmd, body=%wide.region_6.9_spmd.sunk | while | flops 846395392 | bytes 51779372 | solution.py:130
  60.4 4.4 fusion.122
  75.2 4.4 fusion.122
  86.2 25.7 %reduce-scatter.5.cloned.1.call-done = bf16[512,768]{1,0:T(8,128)(2,1)} async-done(((bf16[1024,768]{1,0:T(8,128)(2,1)}), bf16[512,768]{1,0:T(8,128)(2,1)}) %reduce-scatter.5.cloned.1.call-update) | async-done | bytes 786448 | tf_op jit(solution)/shard_map/reduce_scatter | solution.py:132
  119.4 24.2 %all-gather.7.cloned.1.call-done = bf16[1024,768]{1,0:T(8,128)(2,1)} async-done(((bf16[512,768]{1,0:T(8,128)(2,1)}), bf16[1024,768]{1,0:T(8,128)(2,1)}) %all-gather.7.cloned.1.call-update) | async-done | bytes 1572880 | tf_op jit(solution)/shard_map/all_gather | solution.py:144
  143.6 7.4 %fusion.65 = f32[1024,1536]{1,0:T(8,128)} fusion(bf16[1024,768]{1,0:T(8,128)(2,1)} %all-gather.7.cloned.1.call-done, bf16[768,1536]{1,0:T(8,128)(2,1)} %param.38), kind=kOutput, calls=%fused_computation.152 | convolution fusion | flops 2415919104 | bytes 10223616 | tf_op jit(solution)/shard_map/dot_general | solution.py:145
  151.0 21.9 %all-gather.9.cloned.1.call-done = bf16[1024,768]{1,0:T(8,128)(2,1)} async-done(((bf16[512,768]{1,0:T(8,128)(2,1)}), bf16[1024,768]{1,0:T(8,128)(2,1)}) %all-gather.9.cloned.1.call-update) | async-done | bytes 1572880 | tf_op jit(solution)/shard_map/all_gather | solution.py:165
  172.9 20.0 %convert_reduce_fusion = (f32[1536]{0:T(1024)}, bf16[1024,1536]{1,0:T(8,128)(2,1)S(1)}, f32[1024,1536]{1,0:T(8,128)}) fusion(f32[1024,1536]{1,0:T(8,128)} %fusion.65, f32[1536]{0:T(1024)S(1)} %convert_element_type.194, bf16[1024,768]{1,0:T(8,128)(2,1)} %all-gather.9.cloned.1.call-done, bf16[1536,768]{1,0:T(8,128)(2,1)S(1)} %copy-done), kind=kOutput, calls=%fused_computation.49 | convolution fusion | flops 2533882368 | bytes 19673088 | tf_op jit(solution)/shard_map/rd,fd->rf/dot_general | solution.py:169
  194.5 3.7 convolution_convert_fusion.1
  198.3 6.2 multiply_convert_fusion.1
  209.9 14.5 %reduce-scatter.9.cloned.1.call-done = bf16[512,768]{1,0:T(8,128)(2,1)} async-done(((bf16[1024,768]{1,0:T(8,128)(2,1)}), bf16[512,768]{1,0:T(8,128)(2,1)}) %reduce-scatter.9.cloned.1.call-update) | async-done | bytes 786448 | tf_op jit(solution)/shard_map/reduce_scatter | solution.py:174
  229.0 24.3 %reduce-scatter.7.cloned.1.call-done = bf16[512,768]{1,0:T(8,128)(2,1)} async-done(((bf16[1024,768]{1,0:T(8,128)(2,1)}), bf16[512,768]{1,0:T(8,128)(2,1)}) %reduce-scatter.7.cloned.1.call-update) | async-done | bytes 786448 | tf_op jit(solution)/shard_map/reduce_scatter | solution.py:150
  253.3 4.2 multiply_reduce_fusion.2
  260.5 27.3 %all-gather.11.cloned.1.call-done = bf16[1024,768]{1,0:T(8,128)(2,1)} async-done(((bf16[512,768]{1,0:T(8,128)(2,1)}), bf16[1024,768]{1,0:T(8,128)(2,1)}) %all-gather.11.cloned.1.call-update) | async-done | bytes 1572880 | tf_op jit(solution)/shard_map/all_gather | solution.py:191
  291.1 56.1 %while.28 = (s32[]{:T(128)}, f32[1024,6,64]{0,2,1:T(8,128)S(1)}, f32[1024,6,64]{0,2,1:T(8,128)}, bf16[2,512,6,64]{1,3,2,0:T(8,128)(2,1)}, s32[2]{0:T(128)S(1)}, ...) while((s32[]{:T(128)}, f32[1024,6,64]{0,2,1:T(8,128)S(1)}, ...), condition=%wide.region_19.20_spmd.clone, body=%wide.region_17.19_spmd.clone.sunk | while | flops 2075195392 | bytes 132757464 | solution.py:239
  297.1 3.7 bitcast_add_fusion.5
  300.8 7.6 %multiply_reduce_fusion.6 = (f32[6,512]{1,0:T(8,128)S(1)}, f32[6,512,1024]{2,1,0:T(8,128)}) fusion(f32[6,512]{1,0:T(8,128)S(1)} %dynamic-slice_bitcast_fusion.2, f32[6,512,1024]{2,1,0:T(8,128)S(1)} %fusion.132, pred[512,1024]{1,0:T(8,128)(4,1)S(1)} %fusion.134, bf16[1024,6,64]{0,2,1:T(8,128)(2,1)S(1)} %copy-done.27, ...), kind=kOutput, calls=%fused_computation.20.clone.1 | convolution fusion | flops 421524480 | bytes 26898436 | tf_op jit(solution)/shard_map/while/body/eval_jaxpr/qhd,khd->hqk/dot_general | solution.py:220
  308.4 7.3 %multiply_convert_fusion.7 = bf16[6,512,1024]{2,1,0:T(8,128)(2,1)S(1)} fusion(f32[6,512,1024]{2,1,0:T(8,128)} %get-tuple-element.462, f32[6,512]{1,0:T(8,128)S(1)} %get-tuple-element.463, f32[6,512]{1,0:T(8,128)S(1)} %dynamic-slice_bitcast_fusion.2, f32[6,512,1024]{2,1,0:T(8,128)S(1)} %fusion.132, pred[512,1024]{1,0:T(8,128)(4,1)S(1)} %fusion.134), kind=kLoop, calls=%fused_computation.19.clone.1 | loop fusion | flops 22020096 | bytes 32006144 | tf_op jit(solution)/shard_map/while/body/eval_jaxpr/convert_element_type | solution.py:224
  324.9 3.7 bitcast_add_fusion.5
  328.7 7.6 %multiply_reduce_fusion.6 = (f32[6,512]{1,0:T(8,128)S(1)}, f32[6,512,1024]{2,1,0:T(8,128)}) fusion(f32[6,512]{1,0:T(8,128)S(1)} %dynamic-slice_bitcast_fusion.2, f32[6,512,1024]{2,1,0:T(8,128)S(1)} %fusion.132, pred[512,1024]{1,0:T(8,128)(4,1)S(1)} %fusion.134, bf16[1024,6,64]{0,2,1:T(8,128)(2,1)S(1)} %copy-done.27, ...), kind=kOutput, calls=%fused_computation.20.clone.1 | convolution fusion | flops 421524480 | bytes 26898436 | tf_op jit(solution)/shard_map/while/body/eval_jaxpr/qhd,khd->hqk/dot_general | solution.py:220
  336.3 7.3 %multiply_convert_fusion.7 = bf16[6,512,1024]{2,1,0:T(8,128)(2,1)S(1)} fusion(f32[6,512,1024]{2,1,0:T(8,128)} %get-tuple-element.462, f32[6,512]{1,0:T(8,128)S(1)} %get-tuple-element.463, f32[6,512]{1,0:T(8,128)S(1)} %dynamic-slice_bitcast_fusion.2, f32[6,512,1024]{2,1,0:T(8,128)S(1)} %fusion.132, pred[512,1024]{1,0:T(8,128)(4,1)S(1)} %fusion.134), kind=kLoop, calls=%fused_computation.19.clone.1 | loop fusion | flops 22020096 | bytes 32006144 | tf_op jit(solution)/shard_map/while/body/eval_jaxpr/convert_element_type | solution.py:224
  352.4 5.8 bitcast_convert_fusion
  358.2 5.9 fusion.68
  364.2 4.4 fusion.67
  371.1 3.9 convolution_bitcast_fusion.1
  376.5 64.4 %all-reduce.1 = (f32[2,384]{1,0:T(2,128)}, f32[1536]{0:T(1024)}) all-reduce(f32[2,384]{1,0:T(2,128)S(1)} %pad_maximum_fusion.3, f32[1536]{0:T(1024)S(1)} %copy-done.53), channel_id=1, replica_groups=mesh['wide'=16,'narrow'=2] {'wide'}, use_global_device_ids=true, to_apply=%region_32.33 | all-reduce | flops 2304 | bytes 18432 | tf_op jit(solution)/shard_map/psum | solution.py:254
  447.0 39.9 %all-reduce = (f32[768]{0:T(1024)}, f32[768]{0:T(1024)}, f32[768]{0:T(1024)}, f32[768]{0:T(1024)}, f32[768]{0:T(1024)}, /*index=5*/f32[768]{0:T(1024)}, f32[768]{0:T(1024)}, f32[768]{0:T(1024)}, f32[768]{0:T(1024)}) all-reduce(f32[768]{0:T(1024)S(1)} %get-tuple-element.308, ...), channel_id=1, replica_groups=mesh['wide'=16,'narrow'=2] {'wide','narrow'}, use_global_device_ids=true, to_apply=%region_24.25 | all-reduce | flops 6912 | bytes 55296 | tf_op jit(solution)/shard_map/psum | solution.py:280
  489.7 160.6 %all-reduce.5.cloned.1.call-done = (f32[3,768,384]{1,2,0:T(8,128)}, f32[384,768]{1,0:T(8,128)}, f32[768,1536]{1,0:T(8,128)}, f32[1536,768]{1,0:T(8,128)}) async-done(((f32[3,768,384]{1,2,0:T(8,128)}, f32[384,768]{1,0:T(8,128)}, f32[768,1536]{1,0:T(8,128)}, f32[1536,768]{1,0:T(8,128)}), (f32[3,768,384]{1,2,0:T(8,128)}, f32[384,768]{1,0:T(8,128)}, f32[768,1536]{1,0:T(8,128)}, ...) | async-done | bytes 14155792 | tf_op jit(solution)/shard_map/psum | solution.py:254
  650.3 5.2 copy.61
  656.6 5.5 copy.94
  (289 shorter events, 96.4 us)
Async XLA Ops:
  7.2 165.7 %copy-start = (bf16[1536,768]{1,0:T(8,128)(2,1)S(1)}, bf16[1536,768]{1,0:T(8,128)(2,1)}, u32[]{:S(2)}) copy-start(bf16[1536,768]{1,0:T(8,128)(2,1)} %param.40) | copy-start | bytes 7077892
  7.2 6.2 copy-start.2
  7.2 37.8 %all-gather.5.cloned.1.call-start = ((), (), s32[]{:S(2)}) async-start(), calls=%async_computation.4 | async-start | bytes 2359296 | tf_op jit(solution)/shard_map/all_gather | solution.py:98
  8.1 245.1 %copy-start.39 = (pred[512]{0:T(512)(128)(4,1)}, pred[512]{0:T(512)(128)(4,1)S(1)}, u32[]{:S(2)}) copy-start(pred[512]{0:T(512)(128)(4,1)S(1)} %broadcast_compare_fusion) | copy-start | bytes 1540
  8.8 244.4 %copy-start.35 = (f32[768]{0:T(1024)}, f32[768]{0:T(1024)S(1)}, u32[]{:S(2)}) copy-start(f32[768]{0:T(1024)S(1)} %convert_element_type.177) | copy-start | bytes 9220
  12.0 37.1 %copy-start.43 = (f32[512]{0:T(512)}, f32[512]{0:T(512)S(1)}, u32[]{:S(2)}) copy-start(f32[512]{0:T(512)S(1)} %fusion.55) | copy-start | bytes 6148
  14.9 97.0 %reduce-scatter.5.cloned.1.call-start = ((), (), s32[]{:S(2)}) async-start(), calls=%async_computation.5 | async-start | bytes 2359296 | tf_op jit(solution)/shard_map/reduce_scatter | solution.py:132
  85.7 57.8 %all-gather.7.cloned.1.call-start = ((), (), s32[]{:S(2)}) async-start(), calls=%async_computation.6 | async-start | bytes 2359296 | tf_op jit(solution)/shard_map/all_gather | solution.py:144
  116.2 56.7 %all-gather.9.cloned.1.call-start = ((), (), s32[]{:S(2)}) async-start(), calls=%async_computation.8 | async-start | bytes 2359296 | tf_op jit(solution)/shard_map/all_gather | solution.py:165
  119.3 105.2 %reduce-scatter.9.cloned.1.call-start = ((), (), s32[]{:S(2)}) async-start(), calls=%async_computation.9 | async-start | bytes 2359296 | tf_op jit(solution)/shard_map/reduce_scatter | solution.py:174
  172.9 21.6 %copy-start.63 = (bf16[768,1536]{1,0:T(8,128)(2,1)S(1)}, bf16[768,1536]{1,0:T(8,128)(2,1)}, u32[]{:S(2)}) copy-start(bf16[768,1536]{1,0:T(8,128)(2,1)} %param.38) | copy-start | bytes 7077892
  198.2 55.0 %reduce-scatter.7.cloned.1.call-start = ((), (), s32[]{:S(2)}) async-start(), calls=%async_computation.7 | async-start | bytes 2359296 | tf_op jit(solution)/shard_map/reduce_scatter | solution.py:150
  209.8 14.6 %copy-start.4 = (bf16[512,768]{1,0:T(8,128)(2,1)S(1)}, bf16[512,768]{1,0:T(8,128)(2,1)}, u32[]{:S(2)}) copy-start(bf16[512,768]{1,0:T(8,128)(2,1)} %param.24) | copy-start | bytes 2359300
  209.8 14.6 %copy-start.8 = (bf16[512,768]{1,0:T(8,128)(2,1)S(1)}, bf16[512,768]{1,0:T(8,128)(2,1)}, u32[]{:S(2)}) copy-start(bf16[512,768]{1,0:T(8,128)(2,1)} %reduce-scatter.5.cloned.1.call-done) | copy-start | bytes 2359300
  209.9 77.9 %all-gather.11.cloned.1.call-start = ((), (), s32[]{:S(2)}) async-start(), calls=%async_computation.10 | async-start | bytes 2359296 | tf_op jit(solution)/shard_map/all_gather | solution.py:191
  260.4 180.6 %reduce-scatter.11.cloned.1.call-start = ((), (), s32[]{:S(2)}) async-start(), calls=%async_computation.11 | async-start | bytes 2359296 | tf_op jit(solution)/shard_map/reduce_scatter | solution.py:257
  260.4 30.6 %copy-start.6 = (bf16[1024,6,64]{0,2,1:T(8,128)(2,1)S(1)}, bf16[1024,6,64]{0,2,1:T(8,128)(2,1)}, u32[]{:S(2)}) copy-start(bf16[1024,6,64]{0,2,1:T(8,128)(2,1)} %get-tuple-element.588) | copy-start | bytes 2359300
  300.8 7.6 %copy-start.23 = (f32[1024,6,64]{0,2,1:T(8,128)}, f32[1024,6,64]{0,2,1:T(8,128)S(1)}, u32[]{:S(2)}) copy-start(f32[1024,6,64]{0,2,1:T(8,128)S(1)} %bitcast_add_fusion.5) | copy-start | bytes 4718596 | tf_op jit(solution)/shard_map/while
  308.4 7.3 %copy-start.15 = (bf16[2,512,6,64]{1,3,2,0:T(8,128)(2,1)S(1)}, bf16[2,512,6,64]{1,3,2,0:T(8,128)(2,1)}, u32[]{:S(2)}) copy-start(bf16[2,512,6,64]{1,3,2,0:T(8,128)(2,1)} %get-tuple-element.523) | copy-start | bytes 2359300 | tf_op jit(solution)/shard_map/while
  328.6 7.6 %copy-start.23 = (f32[1024,6,64]{0,2,1:T(8,128)}, f32[1024,6,64]{0,2,1:T(8,128)S(1)}, u32[]{:S(2)}) copy-start(f32[1024,6,64]{0,2,1:T(8,128)S(1)} %bitcast_add_fusion.5) | copy-start | bytes 4718596 | tf_op jit(solution)/shard_map/while
  336.3 7.3 %copy-start.15 = (bf16[2,512,6,64]{1,3,2,0:T(8,128)(2,1)S(1)}, bf16[2,512,6,64]{1,3,2,0:T(8,128)(2,1)}, u32[]{:S(2)}) copy-start(bf16[2,512,6,64]{1,3,2,0:T(8,128)(2,1)} %get-tuple-element.523) | copy-start | bytes 2359300 | tf_op jit(solution)/shard_map/while
  358.2 292.2 %all-reduce.5.cloned.1.call-start = ((), (), s32[]{:S(2)}) async-start(), calls=%async_computation.12 | async-start | bytes 28311552 | tf_op jit(solution)/shard_map/psum | solution.py:254
  358.2 5.9 copy-start.20
  375.0 65.9 %copy-start.5 = (bf16[512,768]{1,0:T(8,128)(2,1)S(1)}, bf16[512,768]{1,0:T(8,128)(2,1)}, u32[]{:S(2)}) copy-start(bf16[512,768]{1,0:T(8,128)(2,1)} %param.24) | copy-start | bytes 2359300
  375.0 65.9 %copy-start.36 = (f32[768]{0:T(1024)S(1)}, f32[768]{0:T(1024)}, u32[]{:S(2)}) copy-start(f32[768]{0:T(1024)} %copy-done.35) | copy-start | bytes 9220
  375.0 65.9 %copy-start.38 = (f32[768]{0:T(1024)S(1)}, f32[768]{0:T(1024)}, u32[]{:S(2)}) copy-start(f32[768]{0:T(1024)} %copy-done.37) | copy-start | bytes 9220
  375.0 65.9 %copy-start.40 = (pred[512]{0:T(512)(128)(4,1)S(1)}, pred[512]{0:T(512)(128)(4,1)}, u32[]{:S(2)}) copy-start(pred[512]{0:T(512)(128)(4,1)} %copy-done.39) | copy-start | bytes 1540
  375.0 65.9 %copy-start.42 = (f32[512]{0:T(512)S(1)}, f32[512]{0:T(512)}, u32[]{:S(2)}) copy-start(f32[512]{0:T(512)} %copy-done.41) | copy-start | bytes 6148
  376.1 66.8 %copy-start.46 = (f32[512]{0:T(512)S(1)}, f32[512]{0:T(512)}, u32[]{:S(2)}) copy-start(f32[512]{0:T(512)} %copy-done.45) | copy-start | bytes 6148
  376.1 66.8 %copy-start.44 = (f32[512]{0:T(512)S(1)}, f32[512]{0:T(512)}, u32[]{:S(2)}) copy-start(f32[512]{0:T(512)} %copy-done.43) | copy-start | bytes 6148
  376.3 68.7 %copy-start.10 = (f32[512,768]{1,0:T(8,128)S(1)}, f32[512,768]{1,0:T(8,128)}, u32[]{:S(2)}) copy-start(f32[512,768]{1,0:T(8,128)} %copy-done.9) | copy-start | bytes 4718596
  655.6 6.5 slice-start
  (57 other events, 155.3 us)
Sparse Core Ops, SparseCore 0:
  15.1 29.8 all-gather.4
  85.9 26.0 reduce-scatter.4
  116.3 27.2 all-gather.6
  145.6 27.2 all-gather.8
  198.4 26.0 reduce-scatter.8
  227.2 26.0 reduce-scatter.6
  260.5 27.2 all-gather.10
  358.3 26.0 reduce-scatter.10
  390.1 260.1 all-reduce.4
where the time goes:
time: 681 us; the launch traced here: 672 us
  waiting for transfers between devices  328 us (48%)
  matrix products  115 us (17%)
  blocking collectives  104 us (15%)
  other arithmetic  68.1 us (10%)
  local copies, waits for them, and re-layouts  34.9 us (5%)
  between operations  15 us (2%)
    psum x1, waiting for transfers between devices, shards(): lax.psum((grad_qkv, grad_qv_bias, grad_proj, grad_fc1, grad_fc1_bias, gra...  161 us
    psum x1, blocking collectives, shards(): lax.psum((grad_qkv, grad_qv_bias, grad_proj, grad_fc1, grad_fc1_bias, gra...  64.4 us
    psum x1, blocking collectives, shards(): lax.psum((grad_mask_token, grad_norm1_gain, grad_norm1_bias, grad_proj_bi...  39.9 us
    all_gather x1, waiting for transfers between devices, shards(): normed1_all = lax.all_gather(normed1, 'narrow', axis=0, tiled=True)  29.3 us
    all_gather x1, waiting for transfers between devices, shards(): grad_attn_all = lax.all_gather(grad_attn, 'narrow', axis=0, tiled=True)  27.3 us
    reduce_scatter x1, waiting for transfers between devices, shards(): lax.psum_scatter(jnp.dot(slab(heads_out, jnp.int32(0), own_rows * lax.axi...  25.7 us
    reduce_scatter x1, waiting for transfers between devices, shards(): lax.psum_scatter(jnp.dot(slab(activated, jnp.int32(0), own_rows * lax.axi...  24.3 us
    all_gather x1, waiting for transfers between devices, shards(): normed2_all = lax.all_gather(normed2, 'narrow', axis=0, tiled=True)  24.2 us
  transfers between devices with their start and end apart: 9, of which 8 were waited for; matrix products, arithmetic and copies ran while one was open for 7% of the time, Pallas kernels for 0%

commit v1 on v0

--- a/solution.py
+++ b/solution.py
@@ -278,18 +278,21 @@
         grad_fc2_bias,
         grad_scale_mlp,
     ) = lax.psum(
-        (
-            grad_mask_token,
-            grad_norm1_gain,
-            grad_norm1_bias,
-            grad_proj_bias,
-            grad_scale_attn,
-            grad_norm2_gain,
-            grad_norm2_bias,
-            grad_fc2_bias,
-            grad_scale_mlp,
+        lax.psum(
+            (
+                grad_mask_token,
+                grad_norm1_gain,
+                grad_norm1_bias,
+                grad_proj_bias,
+                grad_scale_attn,
+                grad_norm2_gain,
+                grad_norm2_bias,
+                grad_fc2_bias,
+                grad_scale_mlp,
+            ),
+            "narrow",
         ),
-        ("wide", "narrow"),
+        "wide",
     )
     return (
         output,

time: 681 us -> 681 us (level)
  blocking collectives: 104 us -> 71.4 us
  waiting for transfers between devices: 328 us -> 360 us
    psum x1, blocking collectives: 39.9 us -> 7.31 us  [shards(): lax.psum((grad_mask_token, grad_norm1_gain, grad_norm1_bias, grad_proj_bi...]
    psum x1, waiting for transfers between devices: 161 us -> 185 us  [shards(): lax.psum((grad_qkv, grad_qv_bias, grad_proj, grad_fc1, grad_fc1_bias, gra...]
    reduce_scatter x1, waiting for transfers between devices: 0.01 us -> 7.88 us  [shards(): lax.psum_scatter(jnp.einsum('cre,cde->rd', grad_stack, w_qkv, preferred_e...]
  transfers between devices with their start and end apart: 9 -> 9, of which waited for: 8 -> 9; matrix products, arithmetic and copies ran while one was open for 7% -> 7% of each run, Pallas kernels for 0% -> 0%
where the time goes in v1:
time: 681 us; the launch traced here: 672 us
  waiting for transfers between devices  360 us (53%)
  matrix products  114 us (17%)
  blocking collectives  71.4 us (10%)
  other arithmetic  68 us (10%)
  local copies, waits for them, and re-layouts  35 us (5%)
  between operations  15 us (2%)
  loops' own time  7.12 us (1%)
    psum x1, waiting for transfers between devices, shards(): lax.psum((grad_qkv, grad_qv_bias, grad_proj, grad_fc1, grad_fc1_bias, gra...  185 us
    psum x1, blocking collectives, shards(): lax.psum(lax.psum((grad_mask_token, grad_norm1_gain, grad_norm1_bias, gra...  64.1 us
    all_gather x1, waiting for transfers between devices, shards(): normed1_all = lax.all_gather(normed1, 'narrow', axis=0, tiled=True)  29.3 us
    all_gather x1, waiting for transfers between devices, shards(): grad_attn_all = lax.all_gather(grad_attn, 'narrow', axis=0, tiled=True)  27.3 us
    reduce_scatter x1, waiting for transfers between devices, shards(): lax.psum_scatter(jnp.dot(slab(heads_out, jnp.int32(0), own_rows * lax.axi...  25.8 us
    reduce_scatter x1, waiting for transfers between devices, shards(): lax.psum_scatter(jnp.dot(slab(activated, jnp.int32(0), own_rows * lax.axi...  24.3 us
    all_gather x1, waiting for transfers between devices, shards(): normed2_all = lax.all_gather(normed2, 'narrow', axis=0, tiled=True)  24.2 us
    unnamed x129, local copies, waits for them, and re-layouts  22.7 us
  transfers between devices with their start and end apart: 9, of which 9 were waited for; matrix products, arithmetic and copies ran while one was open for 7% of the time, Pallas kernels for 0%

profile of v1, /device:TPU:0, one launch (start us, length us, event | category | flops | bytes accessed | tf_op | source)
XLA Modules:
  0.0 671.9 jit_solution(10740765388859022304)
XLA Ops:
  15.7 29.3 %all-gather.5.cloned.1.call-done = bf16[1024,768]{1,0:T(8,128)(2,1)} async-done(((bf16[512,768]{1,0:T(8,128)(2,1)}), bf16[1024,768]{1,0:T(8,128)(2,1)}) %all-gather.5.cloned.1.call-update) | async-done | bytes 1572880 | tf_op jit(solution)/shard_map/all_gather | solution.py:98
  45.0 4.0 convolution_bitcast_fusion
  51.0 29.5 %while.27 = (s32[]{:T(128)}, bf16[2,512,6,64]{1,3,2,0:T(8,128)(2,1)}, f32[2,6,512]{2,1,0:T(8,128)S(1)}, s32[2]{0:T(128)S(1)}, s32[1024]{0:T(1024)S(1)}, /*index=...) while((s32[]{:T(128)}, ...), condition=%wide.region_9.10_spmd, body=%wide.region_6.9_spmd.sunk | while | flops 846395392 | bytes 51779372 | solution.py:130
  60.4 4.4 fusion.122
  75.2 4.4 fusion.122
  86.2 25.8 %reduce-scatter.5.cloned.1.call-done = bf16[512,768]{1,0:T(8,128)(2,1)} async-done(((bf16[1024,768]{1,0:T(8,128)(2,1)}), bf16[512,768]{1,0:T(8,128)(2,1)}) %reduce-scatter.5.cloned.1.call-update) | async-done | bytes 786448 | tf_op jit(solution)/shard_map/reduce_scatter | solution.py:132
  119.4 24.2 %all-gather.7.cloned.1.call-done = bf16[1024,768]{1,0:T(8,128)(2,1)} async-done(((bf16[512,768]{1,0:T(8,128)(2,1)}), bf16[1024,768]{1,0:T(8,128)(2,1)}) %all-gather.7.cloned.1.call-update) | async-done | bytes 1572880 | tf_op jit(solution)/shard_map/all_gather | solution.py:144
  143.6 7.4 %fusion.65 = f32[1024,1536]{1,0:T(8,128)} fusion(bf16[1024,768]{1,0:T(8,128)(2,1)} %all-gather.7.cloned.1.call-done, bf16[768,1536]{1,0:T(8,128)(2,1)} %param.38), kind=kOutput, calls=%fused_computation.152 | convolution fusion | flops 2415919104 | bytes 10223616 | tf_op jit(solution)/shard_map/dot_general | solution.py:145
  151.0 21.9 %all-gather.9.cloned.1.call-done = bf16[1024,768]{1,0:T(8,128)(2,1)} async-done(((bf16[512,768]{1,0:T(8,128)(2,1)}), bf16[1024,768]{1,0:T(8,128)(2,1)}) %all-gather.9.cloned.1.call-update) | async-done | bytes 1572880 | tf_op jit(solution)/shard_map/all_gather | solution.py:165
  172.9 20.0 %convert_reduce_fusion = (f32[1536]{0:T(1024)}, bf16[1024,1536]{1,0:T(8,128)(2,1)S(1)}, f32[1024,1536]{1,0:T(8,128)}) fusion(f32[1024,1536]{1,0:T(8,128)} %fusion.65, f32[1536]{0:T(1024)S(1)} %convert_element_type.194, bf16[1024,768]{1,0:T(8,128)(2,1)} %all-gather.9.cloned.1.call-done, bf16[1536,768]{1,0:T(8,128)(2,1)S(1)} %copy-done), kind=kOutput, calls=%fused_computation.49 | convolution fusion | flops 2533882368 | bytes 19673088 | tf_op jit(solution)/shard_map/rd,fd->rf/dot_general | solution.py:169
  194.5 3.7 convolution_convert_fusion.1
  198.3 6.2 multiply_convert_fusion.1
  209.9 14.5 %reduce-scatter.9.cloned.1.call-done = bf16[512,768]{1,0:T(8,128)(2,1)} async-done(((bf16[1024,768]{1,0:T(8,128)(2,1)}), bf16[512,768]{1,0:T(8,128)(2,1)}) %reduce-scatter.9.cloned.1.call-update) | async-done | bytes 786448 | tf_op jit(solution)/shard_map/reduce_scatter | solution.py:174
  228.9 24.3 %reduce-scatter.7.cloned.1.call-done = bf16[512,768]{1,0:T(8,128)(2,1)} async-done(((bf16[1024,768]{1,0:T(8,128)(2,1)}), bf16[512,768]{1,0:T(8,128)(2,1)}) %reduce-scatter.7.cloned.1.call-update) | async-done | bytes 786448 | tf_op jit(solution)/shard_map/reduce_scatter | solution.py:150
  253.3 4.2 multiply_reduce_fusion.2
  260.4 27.3 %all-gather.11.cloned.1.call-done = bf16[1024,768]{1,0:T(8,128)(2,1)} async-done(((bf16[512,768]{1,0:T(8,128)(2,1)}), bf16[1024,768]{1,0:T(8,128)(2,1)}) %all-gather.11.cloned.1.call-update) | async-done | bytes 1572880 | tf_op jit(solution)/shard_map/all_gather | solution.py:191
  291.0 56.5 %while.28 = (s32[]{:T(128)}, f32[1024,6,64]{0,2,1:T(8,128)S(1)}, f32[1024,6,64]{0,2,1:T(8,128)}, bf16[2,512,6,64]{1,3,2,0:T(8,128)(2,1)}, s32[2]{0:T(128)S(1)}, ...) while((s32[]{:T(128)}, f32[1024,6,64]{0,2,1:T(8,128)S(1)}, ...), condition=%wide.region_19.20_spmd.clone, body=%wide.region_17.19_spmd.clone.sunk | while | flops 2075195392 | bytes 132757464 | solution.py:239
  301.1 7.5 %multiply_reduce_fusion.6 = (f32[6,512]{1,0:T(8,128)S(1)}, f32[6,512,1024]{2,1,0:T(8,128)}) fusion(f32[6,512]{1,0:T(8,128)S(1)} %dynamic-slice_bitcast_fusion.2, f32[6,512,1024]{2,1,0:T(8,128)S(1)} %fusion.132, pred[512,1024]{1,0:T(8,128)(4,1)S(1)} %fusion.134, bf16[1024,6,64]{0,2,1:T(8,128)(2,1)S(1)} %copy-done.27, ...), kind=kOutput, calls=%fused_computation.20.clone.1 | convolution fusion | flops 421524480 | bytes 26898436 | tf_op jit(solution)/shard_map/while/body/eval_jaxpr/qhd,khd->hqk/dot_general | solution.py:220
  308.5 7.3 %multiply_convert_fusion.7 = bf16[6,512,1024]{2,1,0:T(8,128)(2,1)S(1)} fusion(f32[6,512,1024]{2,1,0:T(8,128)} %get-tuple-element.471, f32[6,512]{1,0:T(8,128)S(1)} %get-tuple-element.472, f32[6,512]{1,0:T(8,128)S(1)} %dynamic-slice_bitcast_fusion.2, f32[6,512,1024]{2,1,0:T(8,128)S(1)} %fusion.132, pred[512,1024]{1,0:T(8,128)(4,1)S(1)} %fusion.134), kind=kLoop, calls=%fused_computation.19.clone.1 | loop fusion | flops 22020096 | bytes 32006144 | tf_op jit(solution)/shard_map/while/body/eval_jaxpr/convert_element_type | solution.py:224
  325.4 3.7 bitcast_add_fusion.5
  329.2 7.5 %multiply_reduce_fusion.6 = (f32[6,512]{1,0:T(8,128)S(1)}, f32[6,512,1024]{2,1,0:T(8,128)}) fusion(f32[6,512]{1,0:T(8,128)S(1)} %dynamic-slice_bitcast_fusion.2, f32[6,512,1024]{2,1,0:T(8,128)S(1)} %fusion.132, pred[512,1024]{1,0:T(8,128)(4,1)S(1)} %fusion.134, bf16[1024,6,64]{0,2,1:T(8,128)(2,1)S(1)} %copy-done.27, ...), kind=kOutput, calls=%fused_computation.20.clone.1 | convolution fusion | flops 421524480 | bytes 26898436 | tf_op jit(solution)/shard_map/while/body/eval_jaxpr/qhd,khd->hqk/dot_general | solution.py:220
  336.6 7.3 %multiply_convert_fusion.7 = bf16[6,512,1024]{2,1,0:T(8,128)(2,1)S(1)} fusion(f32[6,512,1024]{2,1,0:T(8,128)} %get-tuple-element.471, f32[6,512]{1,0:T(8,128)S(1)} %get-tuple-element.472, f32[6,512]{1,0:T(8,128)S(1)} %dynamic-slice_bitcast_fusion.2, f32[6,512,1024]{2,1,0:T(8,128)S(1)} %fusion.132, pred[512,1024]{1,0:T(8,128)(4,1)S(1)} %fusion.134), kind=kLoop, calls=%fused_computation.19.clone.1 | loop fusion | flops 22020096 | bytes 32006144 | tf_op jit(solution)/shard_map/while/body/eval_jaxpr/convert_element_type | solution.py:224
  352.7 5.8 bitcast_convert_fusion
  358.6 5.9 fusion.68
  364.5 4.4 fusion.67
  371.5 3.9 convolution_bitcast_fusion.1
  376.9 7.9 %reduce-scatter.11.cloned.1.call-done = bf16[512,768]{1,0:T(8,128)(2,1)} async-done(((bf16[1024,768]{1,0:T(8,128)(2,1)}), bf16[512,768]{1,0:T(8,128)(2,1)}) %reduce-scatter.11.cloned.1.call-update) | async-done | bytes 786448 | tf_op jit(solution)/shard_map/reduce_scatter | solution.py:257
  390.8 7.3 %all-reduce.2 = (f32[768]{0:T(1024)S(1)}, f32[768]{0:T(1024)S(1)}, f32[768]{0:T(1024)S(1)}, f32[768]{0:T(1024)S(1)}, f32[768]{0:T(1024)S(1)}, /*index=5*/f32[768...) all-reduce(f32[768]{0:T(1024)S(1)} %get-tuple-element.317, ...), channel_id=1, replica_groups=mesh['wide'=16,'narrow'=2] {'narrow'}, use_global_device_ids=true, to_apply=%region_24.25 | all-reduce | flops 6912 | bytes 55296 | tf_op jit(solution)/shard_map/psum | solution.py:281
  398.2 64.1 %all-reduce = (f32[768]{0:T(1024)}, f32[768]{0:T(1024)}, f32[768]{0:T(1024)}, f32[2,384]{1,0:T(2,128)}, f32[768]{0:T(1024)}, /*index=5*/f32[768]{0:T(1024)}, f32...) all-reduce(f32[768]{0:T(1024)S(1)} %get-tuple-element.293, ...), channel_id=1, replica_groups=mesh['wide'=16,'narrow'=2] {'wide'}, use_global_device_ids=true, to_apply=%region_25.26 | all-reduce | flops 9216 | bytes 73728 | tf_op jit(solution)/shard_map/psum | solution.py:280
  465.0 184.9 %all-reduce.5.cloned.1.call-done = (f32[3,768,384]{1,2,0:T(8,128)}, f32[384,768]{1,0:T(8,128)}, f32[768,1536]{1,0:T(8,128)}, f32[1536,768]{1,0:T(8,128)}) async-done(((f32[3,768,384]{1,2,0:T(8,128)}, f32[384,768]{1,0:T(8,128)}, f32[768,1536]{1,0:T(8,128)}, f32[1536,768]{1,0:T(8,128)}), (f32[3,768,384]{1,2,0:T(8,128)}, f32[384,768]{1,0:T(8,128)}, f32[768,1536]{1,0:T(8,128)}, ...) | async-done | bytes 14155792 | tf_op jit(solution)/shard_map/psum | solution.py:254
  649.9 5.2 copy.61
  656.1 5.5 copy.94
  (289 shorter events, 100.1 us)
Async XLA Ops:
  7.2 165.7 %copy-start = (bf16[1536,768]{1,0:T(8,128)(2,1)S(1)}, bf16[1536,768]{1,0:T(8,128)(2,1)}, u32[]{:S(2)}) copy-start(bf16[1536,768]{1,0:T(8,128)(2,1)} %param.40) | copy-start | bytes 7077892
  7.2 6.2 copy-start.2
  7.2 37.8 %all-gather.5.cloned.1.call-start = ((), (), s32[]{:S(2)}) async-start(), calls=%async_computation.4 | async-start | bytes 2359296 | tf_op jit(solution)/shard_map/all_gather | solution.py:98
  8.1 245.1 %copy-start.39 = (pred[512]{0:T(512)(128)(4,1)}, pred[512]{0:T(512)(128)(4,1)S(1)}, u32[]{:S(2)}) copy-start(pred[512]{0:T(512)(128)(4,1)S(1)} %broadcast_compare_fusion) | copy-start | bytes 1540
  8.9 244.4 %copy-start.35 = (f32[768]{0:T(1024)}, f32[768]{0:T(1024)S(1)}, u32[]{:S(2)}) copy-start(f32[768]{0:T(1024)S(1)} %convert_element_type.177) | copy-start | bytes 9220
  12.0 37.1 %copy-start.43 = (f32[512]{0:T(512)}, f32[512]{0:T(512)S(1)}, u32[]{:S(2)}) copy-start(f32[512]{0:T(512)S(1)} %fusion.55) | copy-start | bytes 6148
  15.0 97.0 %reduce-scatter.5.cloned.1.call-start = ((), (), s32[]{:S(2)}) async-start(), calls=%async_computation.5 | async-start | bytes 2359296 | tf_op jit(solution)/shard_map/reduce_scatter | solution.py:132
  85.7 57.9 %all-gather.7.cloned.1.call-start = ((), (), s32[]{:S(2)}) async-start(), calls=%async_computation.6 | async-start | bytes 2359296 | tf_op jit(solution)/shard_map/all_gather | solution.py:144
  116.2 56.7 %all-gather.9.cloned.1.call-start = ((), (), s32[]{:S(2)}) async-start(), calls=%async_computation.8 | async-start | bytes 2359296 | tf_op jit(solution)/shard_map/all_gather | solution.py:165
  119.3 105.2 %reduce-scatter.9.cloned.1.call-start = ((), (), s32[]{:S(2)}) async-start(), calls=%async_computation.9 | async-start | bytes 2359296 | tf_op jit(solution)/shard_map/reduce_scatter | solution.py:174
  172.9 21.6 %copy-start.63 = (bf16[768,1536]{1,0:T(8,128)(2,1)S(1)}, bf16[768,1536]{1,0:T(8,128)(2,1)}, u32[]{:S(2)}) copy-start(bf16[768,1536]{1,0:T(8,128)(2,1)} %param.38) | copy-start | bytes 7077892
  198.3 55.0 %reduce-scatter.7.cloned.1.call-start = ((), (), s32[]{:S(2)}) async-start(), calls=%async_computation.7 | async-start | bytes 2359296 | tf_op jit(solution)/shard_map/reduce_scatter | solution.py:150
  209.8 14.6 %copy-start.4 = (bf16[512,768]{1,0:T(8,128)(2,1)S(1)}, bf16[512,768]{1,0:T(8,128)(2,1)}, u32[]{:S(2)}) copy-start(bf16[512,768]{1,0:T(8,128)(2,1)} %param.24) | copy-start | bytes 2359300
  209.8 14.6 %copy-start.8 = (bf16[512,768]{1,0:T(8,128)(2,1)S(1)}, bf16[512,768]{1,0:T(8,128)(2,1)}, u32[]{:S(2)}) copy-start(bf16[512,768]{1,0:T(8,128)(2,1)} %reduce-scatter.5.cloned.1.call-done) | copy-start | bytes 2359300
  209.9 77.8 %all-gather.11.cloned.1.call-start = ((), (), s32[]{:S(2)}) async-start(), calls=%async_computation.10 | async-start | bytes 2359296 | tf_op jit(solution)/shard_map/all_gather | solution.py:191
  260.3 124.4 %reduce-scatter.11.cloned.1.call-start = ((), (), s32[]{:S(2)}) async-start(), calls=%async_computation.11 | async-start | bytes 2359296 | tf_op jit(solution)/shard_map/reduce_scatter | solution.py:257
  260.4 30.6 %copy-start.6 = (bf16[1024,6,64]{0,2,1:T(8,128)(2,1)S(1)}, bf16[1024,6,64]{0,2,1:T(8,128)(2,1)}, u32[]{:S(2)}) copy-start(bf16[1024,6,64]{0,2,1:T(8,128)(2,1)} %get-tuple-element.597) | copy-start | bytes 2359300
  301.0 7.5 %copy-start.23 = (f32[1024,6,64]{0,2,1:T(8,128)}, f32[1024,6,64]{0,2,1:T(8,128)S(1)}, u32[]{:S(2)}) copy-start(f32[1024,6,64]{0,2,1:T(8,128)S(1)} %bitcast_add_fusion.5) | copy-start | bytes 4718596 | tf_op jit(solution)/shard_map/while
  308.5 7.3 %copy-start.15 = (bf16[2,512,6,64]{1,3,2,0:T(8,128)(2,1)S(1)}, bf16[2,512,6,64]{1,3,2,0:T(8,128)(2,1)}, u32[]{:S(2)}) copy-start(bf16[2,512,6,64]{1,3,2,0:T(8,128)(2,1)} %get-tuple-element.532) | copy-start | bytes 2359300 | tf_op jit(solution)/shard_map/while
  329.1 7.5 %copy-start.23 = (f32[1024,6,64]{0,2,1:T(8,128)}, f32[1024,6,64]{0,2,1:T(8,128)S(1)}, u32[]{:S(2)}) copy-start(f32[1024,6,64]{0,2,1:T(8,128)S(1)} %bitcast_add_fusion.5) | copy-start | bytes 4718596 | tf_op jit(solution)/shard_map/while
  336.6 7.3 %copy-start.15 = (bf16[2,512,6,64]{1,3,2,0:T(8,128)(2,1)S(1)}, bf16[2,512,6,64]{1,3,2,0:T(8,128)(2,1)}, u32[]{:S(2)}) copy-start(bf16[2,512,6,64]{1,3,2,0:T(8,128)(2,1)} %get-tuple-element.532) | copy-start | bytes 2359300 | tf_op jit(solution)/shard_map/while
  358.5 291.3 %all-reduce.5.cloned.1.call-start = ((), (), s32[]{:S(2)}) async-start(), calls=%async_computation.12 | async-start | bytes 28311552 | tf_op jit(solution)/shard_map/psum | solution.py:254
  375.4 9.4 %copy-start.5 = (bf16[512,768]{1,0:T(8,128)(2,1)S(1)}, bf16[512,768]{1,0:T(8,128)(2,1)}, u32[]{:S(2)}) copy-start(bf16[512,768]{1,0:T(8,128)(2,1)} %param.24) | copy-start | bytes 2359300
  375.4 9.4 %copy-start.36 = (f32[768]{0:T(1024)S(1)}, f32[768]{0:T(1024)}, u32[]{:S(2)}) copy-start(f32[768]{0:T(1024)} %copy-done.35) | copy-start | bytes 9220
  375.4 9.4 %copy-start.38 = (f32[768]{0:T(1024)S(1)}, f32[768]{0:T(1024)}, u32[]{:S(2)}) copy-start(f32[768]{0:T(1024)} %copy-done.37) | copy-start | bytes 9220
  375.4 9.4 %copy-start.40 = (pred[512]{0:T(512)(128)(4,1)S(1)}, pred[512]{0:T(512)(128)(4,1)}, u32[]{:S(2)}) copy-start(pred[512]{0:T(512)(128)(4,1)} %copy-done.39) | copy-start | bytes 1540
  375.4 9.4 %copy-start.42 = (f32[512]{0:T(512)S(1)}, f32[512]{0:T(512)}, u32[]{:S(2)}) copy-start(f32[512]{0:T(512)} %copy-done.41) | copy-start | bytes 6148
  376.5 10.2 %copy-start.46 = (f32[512]{0:T(512)S(1)}, f32[512]{0:T(512)}, u32[]{:S(2)}) copy-start(f32[512]{0:T(512)} %copy-done.45) | copy-start | bytes 6148
  376.5 10.2 %copy-start.44 = (f32[512]{0:T(512)S(1)}, f32[512]{0:T(512)}, u32[]{:S(2)}) copy-start(f32[512]{0:T(512)} %copy-done.43) | copy-start | bytes 6148
  376.7 12.2 %copy-start.10 = (f32[512,768]{1,0:T(8,128)S(1)}, f32[512,768]{1,0:T(8,128)}, u32[]{:S(2)}) copy-start(f32[512,768]{1,0:T(8,128)} %copy-done.9) | copy-start | bytes 4718596
  389.0 9.2 %copy-start.53 = (f32[1536]{0:T(1024)S(1)}, f32[1536]{0:T(1024)}, u32[]{:S(2)}) copy-start(f32[1536]{0:T(1024)} %get-tuple-element.306) | copy-start | bytes 18436
  655.1 6.5 slice-start
  (57 other events, 159.8 us)
Sparse Core Ops, SparseCore 0:
  15.1 29.8 all-gather.4
  85.8 26.0 reduce-scatter.4
  116.3 27.2 all-gather.6
  145.6 27.2 all-gather.8
  198.4 26.0 reduce-scatter.8
  227.1 26.0 reduce-scatter.6
  260.5 27.2 all-gather.10
  358.7 26.0 reduce-scatter.10
  390.5 259.3 all-reduce.4
